TPU v7x, 256 devices: a whole 4x4x8 slice. The times are simulated.
256 devices in a mesh: dp: 4 (over y), ctx: 64 (over z, x, core).
Axes of the slice: x: 4, y: 4, z: 8, core: 2. Of those that a mesh axis runs over, the one named last changes fastest.
Arguments:
- queries: bfloat16 [32768, 2048], P(('dp', 'ctx')), parts along dimension 0, may hold values from -6 to 6
- keys: bfloat16 [32768, 2048], P(('dp', 'ctx')), parts along dimension 0, may hold values from -6 to 6
- values_in: bfloat16 [32768, 2048], P(('dp', 'ctx')), parts along dimension 0, may hold values from -6 to 6
- conv_weights: float32 [4, 6144], replicated, may hold values from -3 to 3
- log_gates: float32 [16, 32768], P(None, ('dp', 'ctx')), parts along dimension 1, may hold values from -0.7 to 0
- betas: float32 [16, 32768], P(None, ('dp', 'ctx')), parts along dimension 1, may hold values from 0 to 0.9
- level_weights: float32 [7, 16, 32768], P(None, None, ('dp', 'ctx')), parts along dimension 2, may hold values from 0.1 to 4
- doc_lengths: int32 [24], P('dp'), parts along dimension 0, may hold values from 1 to 4096, 8192 in all
- out_gain: float32 [2048], replicated, may hold values from 0.1 to 1.9
Outputs:
- mixed: bfloat16 [32768, 2048], P(('dp', 'ctx')), parts along dimension 0
There are 4 independent parts, one for each index of `dp`. A program takes and returns all parts, laid end to end along the dimension named above; an argument that names none is the same for every part. Nothing has to cross between parts.
Inputs may be any that keep to these rules, and one draw needn't show every extreme that they name: `doc_lengths`: the documents tile the 8192 tokens of a sequence; the longest has exactly 4096 tokens.
All inputs are finite; a program needn't handle non-finite values.
Results may differ from a plain program's by a relative error of at most 0.0011.
Values may be sent and summed in bfloat16 or wider, within the bound.
A program may use at most 64 MiB of HBM per device.

v0:
```python
import jax
import jax.numpy as jnp
from jax import lax
from jax.sharding import PartitionSpec as P

DK = 128
LEVELS = 7


def passed_along(x, axis, by):
    peers = lax.axis_size(axis)
    pairs = [(i, i + by) for i in range(peers) if 0 <= i + by < peers]
    return lax.ppermute(x, axis, pairs)


def swapped(block, axis, bit):
    count = lax.axis_size(axis)
    route = []
    for low in range(count):
        high = low | 1 << bit
        if high != low and high < count:
            route += [(low, high), (high, low)]
    return lax.ppermute(block, axis, route)


def tap_mask(starts, first_pos, count, taps):
    extent = first_pos - (taps - 1) + jnp.arange(count + taps - 1, dtype=jnp.int32)
    doc_ext = jnp.sum((starts[None, :] <= extent[:, None]).astype(jnp.int32), axis=1) - 1
    target = doc_ext[taps - 1 :]
    columns = [
        (doc_ext[taps - 1 - offset : taps - 1 - offset + count] == target).astype(jnp.float32)
        for offset in range(taps)
    ]
    return jnp.stack(columns, axis=1)


def reset_flags(starts, first_pos, count):
    position = first_pos + jnp.arange(count, dtype=jnp.int32)
    return jnp.any(position[:, None] == starts[None, :], axis=1).astype(jnp.float32)


def conv_silu(extended, weights, valid):
    taps = weights.shape[0]
    count = valid.shape[0]
    total = jnp.zeros((count, extended.shape[1]), jnp.float32)
    for offset in range(taps):
        rows = extended[taps - 1 - offset : taps - 1 - offset + count].astype(jnp.float32)
        total = total + weights[offset][None, :] * rows * valid[:, offset : offset + 1]
    return jax.nn.silu(total)


def split_heads(flat, heads):
    return flat.reshape(flat.shape[0], heads, -1).transpose(1, 0, 2)


def unit_rows(matrix):
    return matrix * lax.rsqrt(jnp.sum(matrix * matrix, axis=-1, keepdims=True) + 1e-06)


def solve_lower(system, rhs):
    return jax.scipy.linalg.solve_triangular(system, rhs, lower=True, unit_diagonal=True)


def slab_terms(qnorm, knorm, values, gates, strengths, resets):
    count = qnorm.shape[1]
    width = knorm.shape[2]
    highest = lax.Precision.HIGHEST
    segment = jnp.cumsum(resets)
    rows = jnp.arange(count, dtype=jnp.int32)
    keep = (segment[:, None] == segment[None, :]) & (rows[:, None] >= rows[None, :])
    strict = (rows[:, None] > rows[None, :]).astype(jnp.float32)
    cumulative = jnp.cumsum(gates, axis=1)
    spread = cumulative[:, :, None] - cumulative[:, None, :]
    decay = jnp.where(keep[None], jnp.exp(jnp.where(keep[None], spread, 0.0)), 0.0)
    alive = (segment == 0.0).astype(jnp.float32)
    head_decay = jnp.exp(cumulative) * alive[None, :]
    key_key = jnp.einsum("hti,hsi->hts", knorm, knorm, precision=highest)
    system = (
        jnp.eye(count, dtype=jnp.float32)[None]
        + decay * key_key * strengths[:, :, None] * strict[None]
    )
    rhs_keys = (strengths * head_decay)[:, :, None] * knorm
    rhs_values = strengths[:, :, None] * values
    solved = jax.vmap(solve_lower)(system, jnp.concatenate([rhs_keys, rhs_values], axis=2))
    key_part = solved[:, :, :width]
    value_part = solved[:, :, width:]
    query_key = decay * jnp.einsum("hti,hsi->hts", qnorm, knorm, precision=highest)
    local = jnp.einsum("hts,hsv->htv", query_key, value_part, precision=highest)
    qeff = head_decay[:, :, None] * qnorm - jnp.einsum(
        "hts,hsi->hti", query_key, key_part, precision=highest
    )
    last_row = decay[:, count - 1, :]
    weighted = knorm * last_row[:, :, None]
    trans = head_decay[:, count - 1][:, None, None] * jnp.eye(width, dtype=jnp.float32)[
        None
    ] - jnp.einsum("hsi,hsj->hij", weighted, key_part, precision=highest)
    written = jnp.einsum("hsi,hsv->hiv", weighted, value_part, precision=highest)
    return (local, qeff, trans, written)


def finish(heads_out, gain):
    scaled = heads_out * lax.rsqrt(jnp.mean(heads_out * heads_out, axis=-1, keepdims=True) + 1e-06)
    merged = scaled.transpose(1, 0, 2).reshape(heads_out.shape[1], -1)
    return (merged * gain[None, :]).astype(jnp.bfloat16)


def square_product(left, right):
    return jnp.einsum("hij,hjk->hik", left, right, precision=lax.Precision.HIGHEST)


def row_product(left, right):
    return jnp.einsum("hti,hij->htj", left, right, precision=lax.Precision.HIGHEST)


def body(
    queries, keys, values_in, conv_weights, log_gates, betas, level_weights, doc_lengths, out_gain
):
    count = queries.shape[0]
    taps = conv_weights.shape[0]
    heads = log_gates.shape[0]
    width_k = queries.shape[1]
    slab_index = lax.axis_index("ctx")
    first = slab_index * count
    starts = jnp.cumsum(doc_lengths) - doc_lengths
    rim_q, rim_k, rim_v = passed_along(
        (queries[count - taps + 1 :], keys[count - taps + 1 :], values_in[count - taps + 1 :]),
        "ctx",
        1,
    )
    valid = tap_mask(starts, first, count, taps)
    resets = reset_flags(starts, first, count)
    conv_q = conv_silu(jnp.concatenate([rim_q, queries], axis=0), conv_weights[:, :width_k], valid)
    conv_k = conv_silu(
        jnp.concatenate([rim_k, keys], axis=0), conv_weights[:, width_k : 2 * width_k], valid
    )
    conv_v = conv_silu(
        jnp.concatenate([rim_v, values_in], axis=0), conv_weights[:, 2 * width_k :], valid
    )
    qnorm = unit_rows(split_heads(conv_q, heads)) * DK ** (-0.5)
    knorm = unit_rows(split_heads(conv_k, heads))
    values = split_heads(conv_v, heads)
    local, qeff, trans, written = slab_terms(qnorm, knorm, values, log_gates, betas, resets)
    heads_out = level_weights[0][:, :, None] * local
    bits = lax.axis_size("ctx").bit_length() - 1
    block_trans = trans
    block_write = written
    identity = jnp.broadcast_to(jnp.eye(DK, dtype=jnp.float32)[None], trans.shape)
    prefix = identity
    stored = [jnp.zeros_like(written) for level in range(LEVELS)]
    for shift_bit in range(bits):
        partner_trans, partner_write = swapped((block_trans, block_write), "ctx", shift_bit)
        is_upper = jnp.bitwise_and(jnp.right_shift(slab_index, shift_bit), 1) == 1
        level = min(shift_bit + 1, LEVELS - 1)
        stored[level] = jnp.where(is_upper, square_product(prefix, partner_write), 0.0)
        prefix = jnp.where(is_upper, square_product(prefix, partner_trans), prefix)
        if shift_bit + 1 < bits:
            first_trans = jnp.where(is_upper, partner_trans, block_trans)
            first_write = jnp.where(is_upper, partner_write, block_write)
            second_trans = jnp.where(is_upper, block_trans, partner_trans)
            second_write = jnp.where(is_upper, block_write, partner_write)
            block_trans = square_product(second_trans, first_trans)
            block_write = square_product(second_trans, first_write) + second_write
    for level in range(1, LEVELS):
        heads_out = heads_out + level_weights[level][:, :, None] * row_product(qeff, stored[level])
    return finish(heads_out, out_gain)


def solution(mesh):
    in_specs = (
        P(("dp", "ctx"), None),
        P(("dp", "ctx"), None),
        P(("dp", "ctx"), None),
        P(),
        P(None, ("dp", "ctx")),
        P(None, ("dp", "ctx")),
        P(None, None, ("dp", "ctx")),
        P("dp"),
        P(),
    )
    out_specs = P(("dp", "ctx"), None)
    return jax.shard_map(body, mesh=mesh, in_specs=in_specs, out_specs=out_specs, check_vma=False)
```

profile of v0, /device:TPU:1, one launch (start us, length us, event | category | flops | bytes accessed | tf_op | source)
XLA Modules:
  0.0 477.9 jit_solution(7347589617605856338)
XLA Ops:
  1.9 4.5 collective-permute-start.1
  12.0 3.5 collective-permute-start
  24.9 4.0 divide_multiply_fusion.1
  29.7 3.9 divide_multiply_fusion
  34.0 2.7 fusion.9
  36.7 157.8 %custom-call.4 = f32[16,1,128,128]{2,3,1,0:T(8,128)} custom-call(f32[16,1,128,128]{3,2,1,0:T(8,128)S(1)} %fusion.9), custom_call_target="InvertDiagBlocksLowerTriangular" | custom-call | tf_op jit(solution)/shard_map/vmap(jit(_solve_triangular))/triangular_solve | solution.py:61
  197.8 3.4 convolution_subtract_fusion
  201.2 3.4 fusion.37
  205.4 4.7 divide_multiply_fusion.2
  214.2 3.8 convolution_multiply_fusion.1
  218.0 2.8 fusion.31
  221.8 3.4 convolution_add_fusion.4
  231.5 14.1 %collective-permute-done.6 = f32[16,128,128]{2,1,0:T(8,128)S(1)} collective-permute-done((f32[16,128,128]{2,1,0:T(8,128)S(1)}, f32[16,128,128]{2,1,0:T(8,128)S(1)}, u32[]{:S(2)}, u32[]{:S(2)}) %collective-permute-start.6) | collective-permute-done | bytes 1048608 | tf_op jit(solution)/shard_map/ppermute | solution.py:23
  246.9 3.3 collective-permute-start.8
  250.1 17.9 %collective-permute-done.5 = f32[16,128,128]{2,1,0:T(8,128)S(1)} collective-permute-done((f32[16,128,128]{2,1,0:T(8,128)S(1)}, f32[16,128,128]{2,1,0:T(8,128)S(1)}, u32[]{:S(2)}, u32[]{:S(2)}) %collective-permute-start.5) | collective-permute-done | bytes 1048608 | tf_op jit(solution)/shard_map/ppermute | solution.py:23
  269.4 2.9 collective-permute-start.7
  277.5 15.6 %collective-permute-done.8 = f32[16,128,128]{2,1,0:T(8,128)S(1)} collective-permute-done((f32[16,128,128]{2,1,0:T(8,128)S(1)}, f32[16,128,128]{2,1,0:T(8,128)S(1)}, u32[]{:S(2)}, u32[]{:S(2)}) %collective-permute-start.8) | collective-permute-done | bytes 1048608 | tf_op jit(solution)/shard_map/ppermute | solution.py:23
  296.1 19.5 %collective-permute-done.7 = f32[16,128,128]{2,1,0:T(8,128)S(1)} collective-permute-done((f32[16,128,128]{2,1,0:T(8,128)S(1)}, f32[16,128,128]{2,1,0:T(8,128)S(1)}, u32[]{:S(2)}, u32[]{:S(2)}) %collective-permute-start.7) | collective-permute-done | bytes 1048608 | tf_op jit(solution)/shard_map/ppermute | solution.py:23
  324.2 4.3 collective-permute-start.12
  328.5 29.5 %collective-permute-done.9 = f32[16,128,128]{2,1,0:T(8,128)S(1)} collective-permute-done((f32[16,128,128]{2,1,0:T(8,128)S(1)}, f32[16,128,128]{2,1,0:T(8,128)S(1)}, u32[]{:S(2)}, u32[]{:S(2)}) %collective-permute-start.9) | collective-permute-done | bytes 1048608 | tf_op jit(solution)/shard_map/ppermute | solution.py:23
  366.3 29.6 %collective-permute-done.12 = f32[16,128,128]{2,1,0:T(8,128)S(1)} collective-permute-done((f32[16,128,128]{2,1,0:T(8,128)S(1)}, f32[16,128,128]{2,1,0:T(8,128)S(1)}, u32[]{:S(2)}, u32[]{:S(2)}) %collective-permute-start.12) | collective-permute-done | bytes 1048608 | tf_op jit(solution)/shard_map/ppermute | solution.py:23
  396.0 22.5 %collective-permute-done.11 = f32[16,128,128]{2,1,0:T(8,128)S(1)} collective-permute-done((f32[16,128,128]{2,1,0:T(8,128)S(1)}, f32[16,128,128]{2,1,0:T(8,128)S(1)}, u32[]{:S(2)}, u32[]{:S(2)}) %collective-permute-start.11) | collective-permute-done | bytes 1048608 | tf_op jit(solution)/shard_map/ppermute | solution.py:23
  419.7 3.3 collective-permute-start.13
  428.4 42.9 %collective-permute-done.13 = f32[16,128,128]{2,1,0:T(8,128)S(1)} collective-permute-done((f32[16,128,128]{2,1,0:T(8,128)S(1)}, f32[16,128,128]{2,1,0:T(8,128)S(1)}, u32[]{:S(2)}, u32[]{:S(2)}) %collective-permute-start.13) | collective-permute-done | bytes 1048608 | tf_op jit(solution)/shard_map/ppermute | solution.py:23
  (131 shorter events, 73.5 us)
Async XLA Ops:
  0.0 22.2 %copy-start.3 = (bf16[128,2048]{1,0:T(8,128)(2,1)S(1)}, bf16[128,2048]{1,0:T(8,128)(2,1)}, u32[]{:S(2)}) copy-start(bf16[128,2048]{1,0:T(8,128)(2,1)} %param.10) | copy-start | bytes 1572868
  0.0 19.5 %copy-start.20 = (f32[16,128]{1,0:T(8,128)S(1)}, f32[16,128]{1,0:T(8,128)}, u32[]{:S(2)}) copy-start(f32[16,128]{1,0:T(8,128)} %param.13) | copy-start | bytes 24580
  0.0 20.9 %copy-start.5 = (f32[7,16,128]{2,1,0:T(8,128)S(1)}, f32[7,16,128]{2,1,0:T(8,128)}, u32[]{:S(2)}) copy-start(f32[7,16,128]{2,1,0:T(8,128)} %param.15) | copy-start | bytes 172036
  1.9 23.0 %collective-permute-start.1 = (bf16[3,2048]{0,1:T(8,128)(2,1)}, bf16[3,2048]{0,1:T(8,128)(2,1)}, u32[]{:S(2)}, u32[]{:S(2)}) collective-permute-start(bf16[3,2048]{0,1:T(8,128)(2,1)} %copy.52), channel_id=1, source_target_pairs={{0,1},{1,2},{2,3},{3,4},{4,5},{5,6},{6,7},{7,8},{8,9},{9,10},{10,1... | collective-permute-start | bytes 36872 | tf_op jit(solution)/shard_map/ppermute | solution.py:13
  7.2 15.3 %copy-start.4 = (bf16[128,2048]{1,0:T(8,128)(2,1)S(1)}, bf16[128,2048]{1,0:T(8,128)(2,1)}, u32[]{:S(2)}) copy-start(bf16[128,2048]{1,0:T(8,128)(2,1)} %param.11) | copy-start | bytes 1572868
  8.3 21.4 %collective-permute-start.2 = (bf16[3,2048]{0,1:T(8,128)(2,1)}, bf16[3,2048]{0,1:T(8,128)(2,1)}, u32[]{:S(2)}, u32[]{:S(2)}) collective-permute-start(bf16[3,2048]{0,1:T(8,128)(2,1)} %copy.56), channel_id=1, source_target_pairs={{0,1},{1,2},{2,3},{3,4},{4,5},{5,6},{6,7},{7,8},{8,9},{9,10},{10,1... | collective-permute-start | bytes 36872 | tf_op jit(solution)/shard_map/ppermute | solution.py:13
  12.0 193.3 %collective-permute-start = (bf16[3,2048]{0,1:T(8,128)(2,1)}, bf16[3,2048]{0,1:T(8,128)(2,1)}, u32[]{:S(2)}, u32[]{:S(2)}) collective-permute-start(bf16[3,2048]{0,1:T(8,128)(2,1)} %copy.48), channel_id=1, source_target_pairs={{0,1},{1,2},{2,3},{3,4},{4,5},{5,6},{6,7},{7,8},{8,9},{9,10},{10,1... | collective-permute-start | bytes 36872 | tf_op jit(solution)/shard_map/ppermute | solution.py:13
  20.5 4.3 copy-start.6
  29.7 4.3 copy-start.15
  201.2 4.1 copy-start.1
  204.7 13.3 %collective-permute-start.4 = (f32[16,128,128]{2,1,0:T(8,128)}, f32[16,128,128]{2,1,0:T(8,128)}, u32[]{:S(2)}, u32[]{:S(2)}) collective-permute-start(f32[16,128,128]{2,1,0:T(8,128)} %convolution_subtract_fusion), channel_id=1, source_target_pairs={{0,1},{1,0},{2,3},{3,2},{4,5},{5,4},{6,7},{7,6},{8,9},{9,8},{10,11... | collective-permute-start | bytes 3145736 | tf_op jit(solution)/shard_map/ppermute | solution.py:23
  204.7 17.1 %collective-permute-start.3 = (f32[16,128,128]{2,1,0:T(8,128)}, f32[16,128,128]{2,1,0:T(8,128)}, u32[]{:S(2)}, u32[]{:S(2)}) collective-permute-start(f32[16,128,128]{2,1,0:T(8,128)} %fusion.37), channel_id=1, source_target_pairs={{0,1},{1,0},{2,3},{3,2},{4,5},{5,4},{6,7},{7,6},{8,9},{9,8},{10,11... | collective-permute-start | bytes 3145736 | tf_op jit(solution)/shard_map/ppermute | solution.py:23
  220.8 24.8 %collective-permute-start.6 = (f32[16,128,128]{2,1,0:T(8,128)S(1)}, f32[16,128,128]{2,1,0:T(8,128)S(1)}, u32[]{:S(2)}, u32[]{:S(2)}) collective-permute-start(f32[16,128,128]{2,1,0:T(8,128)S(1)} %fusion.31), channel_id=1, source_target_pairs={{0,2},{2,0},{1,3},{3,1},{4,6},{6,4},{5,7},{7,5},{8,10},{10,8},{9,1... | collective-permute-start | bytes 3145736 | tf_op jit(solution)/shard_map/ppermute | solution.py:23
  225.2 2.5 copy-start
  225.2 42.9 %collective-permute-start.5 = (f32[16,128,128]{2,1,0:T(8,128)S(1)}, f32[16,128,128]{2,1,0:T(8,128)S(1)}, u32[]{:S(2)}, u32[]{:S(2)}) collective-permute-start(f32[16,128,128]{2,1,0:T(8,128)S(1)} %convolution_add_fusion.4), channel_id=1, source_target_pairs={{0,2},{2,0},{1,3},{3,1},{4,6},{6,4},{5,7},{7,5},{8,10},{10,8},{9,1... | collective-permute-start | bytes 3145736 | tf_op jit(solution)/shard_map/ppermute | solution.py:23
  246.9 46.2 %collective-permute-start.8 = (f32[16,128,128]{2,1,0:T(8,128)S(1)}, f32[16,128,128]{2,1,0:T(8,128)S(1)}, u32[]{:S(2)}, u32[]{:S(2)}) collective-permute-start(f32[16,128,128]{2,1,0:T(8,128)S(1)} %fusion.28), channel_id=1, source_target_pairs={{0,4},{4,0},{1,5},{5,1},{2,6},{6,2},{3,7},{7,3},{8,12},{12,8},{9,1... | collective-permute-start | bytes 3145736 | tf_op jit(solution)/shard_map/ppermute | solution.py:23
  269.4 46.2 %collective-permute-start.7 = (f32[16,128,128]{2,1,0:T(8,128)S(1)}, f32[16,128,128]{2,1,0:T(8,128)S(1)}, u32[]{:S(2)}, u32[]{:S(2)}) collective-permute-start(f32[16,128,128]{2,1,0:T(8,128)S(1)} %convolution_add_fusion.3), channel_id=1, source_target_pairs={{0,4},{4,0},{1,5},{5,1},{2,6},{6,2},{3,7},{7,3},{8,12},{12,8},{9,1... | collective-permute-start | bytes 3145736 | tf_op jit(solution)/shard_map/ppermute | solution.py:23
  294.3 28.6 %collective-permute-start.10 = (f32[16,128,128]{2,1,0:T(8,128)S(1)}, f32[16,128,128]{2,1,0:T(8,128)S(1)}, u32[]{:S(2)}, u32[]{:S(2)}) collective-permute-start(f32[16,128,128]{2,1,0:T(8,128)S(1)} %fusion.25), channel_id=1, source_target_pairs={{0,8},{8,0},{1,9},{9,1},{2,10},{10,2},{3,11},{11,3},{4,12},{12,4},... | collective-permute-start | bytes 3145736 | tf_op jit(solution)/shard_map/ppermute | solution.py:23
  316.8 41.2 %collective-permute-start.9 = (f32[16,128,128]{2,1,0:T(8,128)S(1)}, f32[16,128,128]{2,1,0:T(8,128)S(1)}, u32[]{:S(2)}, u32[]{:S(2)}) collective-permute-start(f32[16,128,128]{2,1,0:T(8,128)S(1)} %convolution_add_fusion.2), channel_id=1, source_target_pairs={{0,8},{8,0},{1,9},{9,1},{2,10},{10,2},{3,11},{11,3},{4,12},{12,4},... | collective-permute-start | bytes 3145736 | tf_op jit(solution)/shard_map/ppermute | solution.py:23
  324.2 71.7 %collective-permute-start.12 = (f32[16,128,128]{2,1,0:T(8,128)S(1)}, f32[16,128,128]{2,1,0:T(8,128)S(1)}, u32[]{:S(2)}, u32[]{:S(2)}) collective-permute-start(f32[16,128,128]{2,1,0:T(8,128)S(1)} %fusion.22), channel_id=1, source_target_pairs={{0,16},{16,0},{1,17},{17,1},{2,18},{18,2},{3,19},{19,3},{4,20},{20... | collective-permute-start | bytes 3145736 | tf_op jit(solution)/shard_map/ppermute | solution.py:23
  359.3 59.2 %collective-permute-start.11 = (f32[16,128,128]{2,1,0:T(8,128)S(1)}, f32[16,128,128]{2,1,0:T(8,128)S(1)}, u32[]{:S(2)}, u32[]{:S(2)}) collective-permute-start(f32[16,128,128]{2,1,0:T(8,128)S(1)} %convolution_add_fusion.1), channel_id=1, source_target_pairs={{0,16},{16,0},{1,17},{17,1},{2,18},{18,2},{3,19},{19,3},{4,20},{20... | collective-permute-start | bytes 3145736 | tf_op jit(solution)/shard_map/ppermute | solution.py:23
  419.7 51.6 %collective-permute-start.13 = (f32[16,128,128]{2,1,0:T(8,128)S(1)}, f32[16,128,128]{2,1,0:T(8,128)S(1)}, u32[]{:S(2)}, u32[]{:S(2)}) collective-permute-start(f32[16,128,128]{2,1,0:T(8,128)S(1)} %convolution_add_fusion), channel_id=1, source_target_pairs={{0,32},{32,0},{1,33},{33,1},{2,34},{34,2},{3,35},{35,3},{4,36},{36... | collective-permute-start | bytes 3145736 | tf_op jit(solution)/shard_map/ppermute | solution.py:23
  428.4 44.1 %copy-start.7 = (f32[16,128]{1,0:T(8,128)S(1)}, f32[16,128]{1,0:T(8,128)}, u32[]{:S(2)}) copy-start(f32[16,128]{1,0:T(8,128)} %get-tuple-element.32) | copy-start | bytes 24580
  472.5 2.4 copy-start.8
  (12 other events, 20.4 us)
where the time goes:
time: 481 us; the launch traced here: 478 us
  waiting for transfers between devices  192 us (40%)
  other arithmetic  179 us (37%)
  matrix products  60.5 us (13%)
  starting transfers between devices  30.4 us (6%)
  local copies, waits for them, and re-layouts  15 us (3%)
    ppermute x11, waiting for transfers between devices, swapped(): return lax.ppermute(block, axis, route)  192 us
    another operation x4, other arithmetic, solve_lower(): jax.scipy.linalg.solve_triangular(system, rhs, lower=True, unit_diagonal=...  159 us
    dot_general x20, matrix products, square_product(): jnp.einsum('hij,hjk->hik', left, right, precision=lax.Precision.HIGHEST)  30 us
    ppermute x11, starting transfers between devices, swapped(): return lax.ppermute(block, axis, route)  20.5 us
    mul x3, other arithmetic, conv_silu(): return jax.nn.silu(total)  12.7 us
    dot_general x6, matrix products, row_product(): jnp.einsum('hti,hij->htj', left, right, precision=lax.Precision.HIGHEST)  11.7 us
    ppermute x3, starting transfers between devices, passed_along(): return lax.ppermute(x, axis, pairs)  9.9 us
  transfers between devices with their start and end apart: 14, of which 8 were waited for; matrix products, arithmetic and copies ran while one was open for 51% of the time, Pallas kernels for 0%

commit v1 on v0

v1 whole, which is shorter than its diff:
```python
import functools
import jax
import jax.numpy as jnp
from jax import lax
from jax.experimental import pallas as pl
from jax.experimental.pallas import tpu as pltpu
from jax.sharding import PartitionSpec as P

F32 = jnp.float32
BF16 = jnp.bfloat16
C = 128
SEG = 16
NB = 4


def halves(x):
    high = x.astype(BF16)
    low = (x - high.astype(F32)).astype(BF16)
    return high, low


def left_form(x):
    return jnp.concatenate(halves(x), axis=1)


def right_form(x):
    high, low = halves(x)
    wide = jnp.concatenate([high, low], axis=1)
    return jnp.concatenate([wide, wide], axis=0)


def times(left, right):
    r = jnp.dot(left, right, preferred_element_type=F32)
    return r[:, :C] + r[:, C:]


def lanes_ds(i):
    return pl.ds(pl.multiple_of(i * C, C), C)


def fill_rows(first, doc_ref, scal_ref, rows_ref):
    bounds = []
    acc = jnp.int32(0)
    for i in range(doc_ref.shape[0]):
        bounds.append(acc)
        acc = acc + doc_ref[i]
    pos = first + lax.broadcasted_iota(jnp.int32, (SEG, C), 0) * C + lax.broadcasted_iota(jnp.int32, (SEG, C), 1)
    slab_pos = first + lax.broadcasted_iota(jnp.int32, (SEG, C), 0) * C - 1

    def doc_of(p):
        total = jnp.zeros((SEG, C), F32)
        for b in bounds:
            total = total + jnp.where(p >= b, 1.0, 0.0)
        return total

    doc = doc_of(pos)
    upper = (lax.broadcasted_iota(jnp.int32, (C, C), 0) <= lax.broadcasted_iota(jnp.int32, (C, C), 1)).astype(F32)
    cum = jnp.dot(scal_ref[:, 0, :], upper, precision=lax.Precision.HIGHEST, preferred_element_type=F32)
    rows_ref[:, 0, :] = cum
    rows_ref[:, 1, :] = scal_ref[:, 1, :]
    for l in range(7):
        rows_ref[:, 2 + l, :] = scal_ref[:, 2 + l, :]
    rows_ref[:, 9, :] = doc
    rows_ref[:, 10, :] = jnp.where(doc == doc_of(slab_pos), jnp.exp(cum), 0.0)
    for m in (1, 2, 3):
        rows_ref[:, 10 + m, :] = jnp.where(doc == doc_of(pos - m), 1.0, 0.0)
    rows_ref[:, 14, :] = jnp.zeros((SEG, C), F32)
    rows_ref[:, 15, :] = jnp.zeros((SEG, C), F32)


def conv(ext, taps, valid):
    x = ext.astype(F32)
    total = taps[0:1] * x[16:]
    for m in (1, 2, 3):
        total = total + taps[m : m + 1] * x[16 - m : 144 - m] * valid[m - 1]
    return total / (1.0 + jnp.exp(-total))


def slab_group(js, taps, rows_ref, x_ref, rim_ref, local_ref, qeff_ref, trans_ref, write_ref):
    it = lax.broadcasted_iota(jnp.int32, (C, C), 0)
    js_ = lax.broadcasted_iota(jnp.int32, (C, C), 1)
    lower = it >= js_
    apart = jnp.where(it > js_, it ^ js_, 0)
    eye = jnp.where(it == js_, 1.0, 0.0)
    n = len(js)
    q, k, v, cols, rows = [], [], [], [], []
    for j in js:
        r = rows_ref[j]
        c = r.T
        rows.append(r)
        cols.append(c)
        valid = [c[:, 10 + m : 11 + m] for m in (1, 2, 3)]
        cq, ck, cv = [conv(jnp.concatenate([rim_ref[j, a], x_ref[j, a]], axis=0), taps[a], valid) for a in range(3)]
        q.append(cq * (lax.rsqrt(jnp.sum(cq * cq, axis=1, keepdims=True) + 1e-06) * C ** (-0.5)))
        k.append(ck * lax.rsqrt(jnp.sum(ck * ck, axis=1, keepdims=True) + 1e-06))
        v.append(cv)
    kt = [x.T for x in k]
    gram = [times(left_form(jnp.concatenate([q[i], k[i]], axis=0)), right_form(kt[i])) for i in range(n)]
    outer, system = [], []
    for i in range(n):
        r, c = rows[i], cols[i]
        keep = lower & (c[:, 9:10] == r[9:10])
        decay = jnp.exp(jnp.where(keep, c[:, 0:1] - r[0:1], -1e30))
        beta = r[1:2]
        outer.append(jnp.concatenate([decay * gram[i][:C], kt[i] * decay[C - 1 : C]], axis=0) * beta)
        system.append(decay * gram[i][C:] * beta)
    inverse = [eye - jnp.where(apart == 1, system[i], 0.0) for i in range(n)]
    b = 2
    while b < C:
        pick = (apart >= b) & (apart < 2 * b)
        half = [times(left_form(inverse[i]), right_form(jnp.where(pick, system[i], 0.0))) for i in range(n)]
        inverse = [inverse[i] - times(left_form(half[i]), right_form(inverse[i])) for i in range(n)]
        b *= 2
    mixed = [left_form(times(left_form(outer[i]), right_form(inverse[i]))) for i in range(n)]
    for i in range(n):
        hd = cols[i][:, 10:11]
        with_v = times(mixed[i], right_form(v[i]))
        with_k = times(mixed[i], right_form(k[i] * hd))
        local_ref[js[i]] = with_v[:C] * cols[i][:, 2:3]
        write_ref[js[i]] = with_v[C:]
        qeff_ref[js[i]] = q[i] * hd - with_k[:C]
        trans_ref[js[i]] = rows[i][10:11, C - 1 : C] * eye - with_k[C:]


def scan_half(part, levels, prefix, rows_ref, local_ref, qeff_ref, trans_ref, write_ref, reach_ref):
    for j in range(part * SEG // 2, (part + 1) * SEG // 2):
        trans = trans_ref[j]
        qeff = qeff_ref[j]
        moved = {}
        if j:
            both = left_form(jnp.concatenate([qeff, trans], axis=0))
            c = rows_ref[j].T
            total = local_ref[j]
            for l, state in levels.items():
                r = times(both, right_form(state))
                total = total + r[:C] * c[:, 2 + l : 3 + l]
                moved[l] = r[C:]
            local_ref[j] = total
            r = times(both, right_form(prefix))
            reach_ref[j] = r[:C]
            prefix = r[C:]
        else:
            reach_ref[j] = qeff
            prefix = trans
        target = (j ^ (j + 1)).bit_length()
        merged = write_ref[j]
        for l in list(moved):
            if l <= target:
                merged = merged + moved.pop(l)
        moved[target] = merged
        levels = moved
    return levels, prefix


def block_totals(trans_ref, write_ref, seg_ref):
    blocks = [(trans_ref[j], write_ref[j]) for j in range(SEG)]
    while len(blocks) > 1:
        joined = []
        for a in range(0, len(blocks), 2):
            upper = left_form(blocks[a + 1][0])
            joined.append((
                times(upper, right_form(blocks[a][0])),
                times(upper, right_form(blocks[a][1])) + blocks[a + 1][1],
            ))
        blocks = joined
    seg_ref[0] = blocks[0][0]
    seg_ref[1] = blocks[0][1]


def final(j, s5, s6, gain, rows_ref, local_ref, reach_ref):
    c = rows_ref[j].T
    reach = left_form(reach_ref[j])
    o = local_ref[j] + times(reach, s5) * c[:, 7:8] + times(reach, s6) * c[:, 8:9]
    return (o * lax.rsqrt(jnp.mean(o * o, axis=1, keepdims=True) + 1e-06) * gain).astype(BF16)


def kernel(
    doc_ref, cw_ref, gain_ref, scal_src, q_src, k_src, v_src, out_ref,
    x_ref, rim_ref, scal_ref, rows_ref, local_ref, qeff_ref, trans_ref, write_ref, reach_ref,
    seg_ref, far_ref, joint_ref, states_ref, stage_ref,
    in_send, in_recv, rim_send, rim_recv, far_send, far_recv, out_send, out_recv,
):
    me = lax.axis_index("ctx")
    segment = lax.div(me, SEG)
    mine = lax.rem(me, SEG)
    my_z, my_x, my_core = lax.div(mine, 8), lax.rem(lax.div(mine, 2), 4), lax.rem(mine, 2)

    def place(dz, dx, dc):
        return lax.rem(my_z + dz, 2) * 8 + lax.rem(my_x + dx, 4) * 2 + lax.rem(my_core + dc, 2)

    def at(seg, head):
        return {"ctx": lax.rem(seg, 4) * SEG + head}

    barrier = pltpu.get_barrier_semaphore()

    def greet(target):
        pl.semaphore_signal(barrier, inc=1, device_id=target, device_id_type=pl.DeviceIdType.MESH)

    for n in range(1, SEG):
        greet(at(segment, lax.rem(mine + n, SEG)))
    for n in range(1, 4):
        greet(at(segment + n, mine))
    greet(at(segment + 3, SEG - 1))

    @pl.when(mine == SEG - 1)
    def _():
        for n in range(SEG):
            greet(at(segment + 1, n))
        pl.semaphore_wait(barrier, 19 + SEG)

    @pl.when(mine != SEG - 1)
    def _():
        pl.semaphore_wait(barrier, 19)

    sources = (q_src, k_src, v_src)

    def piece(a, src, dst, head, slab):
        if a == 3:
            return scal_src.at[head], scal_ref.at[slab]
        return sources[a].at[:, lanes_ds(head)], x_ref.at[slab, a]

    def sending(a, head):
        src, dst = piece(a, None, None, head, mine)
        return pltpu.make_async_remote_copy(
            src_ref=src, dst_ref=dst, send_sem=in_send.at[head, a], recv_sem=in_recv.at[mine, a],
            device_id=at(segment, head), device_id_type=pl.DeviceIdType.MESH,
        )

    def keeping(a):
        src, dst = piece(a, None, None, mine, mine)
        return pltpu.make_async_copy(src, dst, in_recv.at[mine, a])

    def arriving(a, slab):
        src, dst = piece(a, None, None, mine, slab)
        return pltpu.make_async_remote_copy(
            src_ref=src, dst_ref=dst, send_sem=in_send.at[slab, a], recv_sem=in_recv.at[slab, a],
            device_id=at(segment, slab), device_id_type=pl.DeviceIdType.MESH,
        )

    follower = lax.rem(mine + 1, SEG)

    def rim(a, head, slot, seg):
        return pltpu.make_async_remote_copy(
            src_ref=sources[a].at[pl.ds(C - 16, 16), lanes_ds(head)], dst_ref=rim_ref.at[slot, a],
            send_sem=rim_send.at[head, a], recv_sem=rim_recv.at[slot, a],
            device_id=at(seg, head), device_id_type=pl.DeviceIdType.MESH,
        )

    def own_rim(a):
        return pltpu.make_async_copy(
            sources[a].at[pl.ds(C - 16, 16), lanes_ds(mine)], rim_ref.at[follower, a], rim_recv.at[follower, a]
        )

    def rims_out(act):
        @pl.when(mine == SEG - 1)
        def _():
            for n in range(SEG):
                for a in range(3):
                    act(rim(a, jnp.int32(n), follower, segment + 1))

        @pl.when(mine != SEG - 1)
        def _():
            for step in order:
                for a in range(3):
                    act(rim(a, place(*step), follower, segment))

    def await_rim(slot):
        local = slot == mine + 1

        @pl.when(local)
        def _():
            for a in range(3):
                own_rim(a).wait()

        @pl.when(jnp.logical_not(local))
        def _():
            for a in range(3):
                rim(a, mine, slot, segment).wait_recv()

    for a in range(4):
        keeping(a).start()
    order = [(dz, dx, dc) for dx in (0, 1, 3, 2) for dz in (0, 1) for dc in (0, 1)][1:]
    for step in order:
        sending(3, place(*step)).start()
    rims_out(lambda copy: copy.start())

    @pl.when(mine != SEG - 1)
    def _():
        for a in range(3):
            own_rim(a).start()

    for step in order:
        for a in range(3):
            sending(a, place(*step)).start()

    keeping(3).wait()
    for step in order:
        arriving(3, place(step[0], (4 - step[1]) % 4, step[2])).wait_recv()
    fill_rows(segment * (SEG * C), doc_ref, scal_ref, rows_ref)
    for a in range(3):
        keeping(a).wait()

    taps = [cw_ref[:, lanes_ds(SEG * a + mine)] for a in range(3)]

    def group(m, _):
        dx = m + lax.div(m, 2) - 2 * lax.div(m, 3)
        js = [place(dz, 4 - dx, dc) for dz in (0, 1) for dc in (0, 1)]
        for n, j in enumerate(js):
            if n:
                for a in range(3):
                    arriving(a, j).wait_recv()
            else:
                @pl.when(m > 0)
                def _():
                    for a in range(3):
                        arriving(a, j).wait_recv()
        for j in js:
            await_rim(j)
        slab_group(js, taps, rows_ref, x_ref, rim_ref, local_ref, qeff_ref, trans_ref, write_ref)
        return 0

    lax.fori_loop(0, SEG // NB, group, 0)

    def across(n, src, to):
        return pltpu.make_async_remote_copy(
            src_ref=src, dst_ref=far_ref.at[n], send_sem=far_send.at[n], recv_sem=far_recv.at[n],
            device_id=at(jnp.int32(to), mine), device_id_type=pl.DeviceIdType.MESH,
        )

    block_totals(trans_ref, write_ref, seg_ref)
    first_write = across(0, seg_ref.at[1], 1)
    third_trans = across(1, seg_ref.at[0], 3)
    third_write = across(2, seg_ref.at[1], 3)
    to_third = across(3, joint_ref, 2)
    to_fourth = pltpu.make_async_remote_copy(
        src_ref=joint_ref, dst_ref=far_ref.at[3], send_sem=far_send.at[4], recv_sem=far_recv.at[3],
        device_id=at(jnp.int32(3), mine), device_id_type=pl.DeviceIdType.MESH,
    )

    @pl.when(segment == 0)
    def _():
        first_write.start()

    @pl.when(segment == 2)
    def _():
        third_trans.start()
        third_write.start()

    levels, prefix = scan_half(0, {}, None, rows_ref, local_ref, qeff_ref, trans_ref, write_ref, reach_ref)

    states_ref[...] = jnp.zeros_like(states_ref)

    @pl.when(segment == 1)
    def _():
        first_write.wait_recv()
        states_ref[0] = far_ref[0]
        joint_ref[...] = times(left_form(seg_ref[0]), right_form(far_ref[0])) + seg_ref[1]
        to_third.start()
        to_fourth.start()

    scan_half(1, levels, prefix, rows_ref, local_ref, qeff_ref, trans_ref, write_ref, reach_ref)

    @pl.when(segment == 2)
    def _():
        to_third.wait_recv()
        states_ref[1] = far_ref[3]

    @pl.when(segment == 3)
    def _():
        third_trans.wait_recv()
        third_write.wait_recv()
        states_ref[0] = far_ref[2]
        to_fourth.wait_recv()
        states_ref[1] = times(left_form(far_ref[1]), right_form(far_ref[3]))

    gain = gain_ref[:, lanes_ds(mine)]
    s5 = right_form(states_ref[0])
    s6 = right_form(states_ref[1])

    def leaving(slab):
        return pltpu.make_async_remote_copy(
            src_ref=stage_ref.at[slab], dst_ref=out_ref.at[:, lanes_ds(mine)],
            send_sem=out_send.at[slab], recv_sem=out_recv.at[mine],
            device_id=at(segment, slab), device_id_type=pl.DeviceIdType.MESH,
        )

    def returning(head):
        return pltpu.make_async_remote_copy(
            src_ref=stage_ref.at[head], dst_ref=out_ref.at[:, lanes_ds(head)],
            send_sem=out_send.at[head], recv_sem=out_recv.at[head],
            device_id=at(segment, head), device_id_type=pl.DeviceIdType.MESH,
        )

    for dx in (2, 1, 3, 0):
        js = [place(dz, dx, dc) for dz in (1, 0) for dc in (1, 0)]
        for j in js:
            stage_ref[j] = final(j, s5, s6, gain, rows_ref, local_ref, reach_ref)
        for j in js[: 4 if dx else 3]:
            leaving(j).start()
    home = pltpu.make_async_copy(stage_ref.at[mine], out_ref.at[:, lanes_ds(mine)], out_recv.at[mine])
    home.start()
    home.wait()
    for step in order:
        returning(place(*step)).wait_recv()

    for step in order:
        head = place(*step)
        for a in range(4):
            sending(a, head).wait_send()
        leaving(head).wait_send()

    rims_out(lambda copy: copy.wait_send())

    @pl.when(segment == 0)
    def _():
        first_write.wait_send()

    @pl.when(segment == 1)
    def _():
        to_third.wait_send()
        to_fourth.wait_send()

    @pl.when(segment == 2)
    def _():
        third_trans.wait_send()
        third_write.wait_send()


def body(queries, keys, values_in, conv_weights, log_gates, betas, level_weights, doc_lengths, out_gain):
    heads, count = log_gates.shape
    scal = jnp.concatenate(
        [log_gates[None], betas[None], level_weights, jnp.zeros((7, heads, count), F32)], axis=0
    ).transpose(1, 0, 2)
    square = pltpu.VMEM((SEG, C, C), F32)
    hbm = pl.BlockSpec(memory_space=pl.ANY)
    vmem = pl.BlockSpec(memory_space=pltpu.VMEM)
    dma = pltpu.SemaphoreType.DMA
    return pl.pallas_call(
        kernel,
        out_shape=jax.ShapeDtypeStruct(queries.shape, BF16),
        in_specs=[pl.BlockSpec(memory_space=pltpu.SMEM), vmem, vmem, hbm, hbm, hbm, hbm],
        out_specs=hbm,
        scratch_shapes=[
            pltpu.VMEM((SEG, 3, C, C), BF16),
            pltpu.VMEM((SEG, 3, 16, C), BF16),
            pltpu.VMEM((SEG, 16, C), F32),
            pltpu.VMEM((SEG, 16, C), F32),
            square, square, square, square, square,
            pltpu.VMEM((2, C, C), F32),
            pltpu.VMEM((4, C, C), F32),
            pltpu.VMEM((C, C), F32),
            pltpu.VMEM((2, C, C), F32),
            pltpu.VMEM((SEG, C, C), BF16),
            dma((SEG, 4)), dma((SEG, 4)), dma((SEG, 3)), dma((SEG, 3)), dma((5,)), dma((4,)), dma((SEG,)), dma((SEG,)),
        ],
        compiler_params=pltpu.CompilerParams(
            collective_id=0, has_side_effects=True, vmem_limit_bytes=48 << 20
        ),
    )(doc_lengths, conv_weights, out_gain[None, :], scal, queries, keys, values_in)


def solution(mesh):
    in_specs = (
        P(("dp", "ctx"), None),
        P(("dp", "ctx"), None),
        P(("dp", "ctx"), None),
        P(),
        P(None, ("dp", "ctx")),
        P(None, ("dp", "ctx")),
        P(None, None, ("dp", "ctx")),
        P("dp"),
        P(),
    )
    out_specs = P(("dp", "ctx"), None)
    return jax.shard_map(body, mesh=mesh, in_specs=in_specs, out_specs=out_specs, check_vma=False)
```

time: 481 us -> 60.6 us (0.13)
  waiting for transfers between devices: 192 us -> 0 us
  other arithmetic: 179 us -> 0.08 us
  matrix products: 60.5 us -> 0 us
  Pallas kernels: 0 us -> 53.6 us
  starting transfers between devices: 30.4 us -> 0 us
  local copies, waits for them, and re-layouts: 15 us -> 5.67 us
    ppermute x14 -> x0, waiting for transfers between devices: 192 us -> none  [the longest x11 192 us: swapped(): return lax.ppermute(block, axis, route)]
    another operation x8 -> x0, other arithmetic: 160 us -> none  [the longest x4 159 us: solve_lower(): jax.scipy.linalg.solve_triangular(system, rhs, lower=True, unit_diagonal=...]
    dot_general x32 -> x0, matrix products: 58.5 us -> none  [the longest x20 30 us: square_product(): jnp.einsum('hij,hjk->hik', left, right, precision=lax.Precision.HIGHEST)]
    pallas_call x0 -> x1, Pallas kernels: none -> 53.6 us  [body(): pl.pallas_call(kernel, out_shape=jax.ShapeDtypeStruct(queries.shape, BF16...]
    ppermute x14 -> x0, starting transfers between devices: 30.4 us -> none  [the longest x11 20.5 us: swapped(): return lax.ppermute(block, axis, route)]
    mul x7 -> x0, other arithmetic: 14.7 us -> none  [the longest x3 12.7 us: conv_silu(): return jax.nn.silu(total)]
    slice x9 -> x0, local copies, waits for them, and re-layouts: 7.46 us -> none  [the longest x2 1.9 us: body(): keys[count - taps + 1:]]
  transfers between devices with their start and end apart: 14 -> 0, of which waited for: 8 -> 0; matrix products, arithmetic and copies ran while one was open for 51% -> 0% of each run, Pallas kernels for 0% -> 0%
where the time goes in v1:
time: 60.6 us; the launch traced here: 59.4 us
  Pallas kernels  53.6 us (88%)
  local copies, waits for them, and re-layouts  5.67 us (9%)
    pallas_call x1, Pallas kernels, body(): pl.pallas_call(kernel, out_shape=jax.ShapeDtypeStruct(queries.shape, BF16...  53.6 us
    unnamed x18, local copies, waits for them, and re-layouts  5.59 us

profile of v1, /device:TPU:1, one launch (start us, length us, event | category | flops | bytes accessed | tf_op | source)
XLA Modules:
  0.0 59.4 jit_solution(12544639810934829668)
XLA Ops:
  0.0 0.1 pad.3.clone
  0.1 0.0 copy-start.6
  0.1 0.0 copy-start.7
  0.1 0.9 %copy.10 = f32[7,16,128]{2,0,1:T(8,128)S(1)} copy(f32[7,16,128]{2,1,0:T(8,128)} %param.15) | data formatting | bytes 114688 | tf_op args[6]
  1.0 0.0 copy-done.6
  1.0 0.0 copy-done.7
  1.0 0.0 copy-start.3
  1.0 0.0 copy-start.4
  1.0 0.0 copy-start.5
  1.0 0.1 maximum_bitcast_fusion.scal_src
  1.1 0.8 %copy-done.3 = f32[4,6144]{1,0:T(4,128)S(1)} copy-done((f32[4,6144]{1,0:T(4,128)S(1)}, f32[4,6144]{1,0:T(4,128)}, u32[]{:S(2)}) %copy-start.3) | copy-done | bytes 98328
  1.9 0.0 copy-done.4
  1.9 0.0 copy-done.5
  1.9 0.0 copy-start
  1.9 1.0 %copy-done = bf16[128,2048]{1,0:T(8,128)(2,1)S(1)} copy-done((bf16[128,2048]{1,0:T(8,128)(2,1)S(1)}, bf16[128,2048]{1,0:T(8,128)(2,1)}, u32[]{:S(2)}) %copy-start) | copy-done | bytes 524312
  2.9 0.0 copy-start.1
  2.9 1.0 %copy-done.1 = bf16[128,2048]{1,0:T(8,128)(2,1)S(1)} copy-done((bf16[128,2048]{1,0:T(8,128)(2,1)S(1)}, bf16[128,2048]{1,0:T(8,128)(2,1)}, u32[]{:S(2)}) %copy-start.1) | copy-done | bytes 524312
  4.0 0.0 copy-start.2
  4.0 1.0 %copy-done.2 = bf16[128,2048]{1,0:T(8,128)(2,1)S(1)} copy-done((bf16[128,2048]{1,0:T(8,128)(2,1)S(1)}, bf16[128,2048]{1,0:T(8,128)(2,1)}, u32[]{:S(2)}) %copy-start.2) | copy-done | bytes 524312
  5.0 53.6 %shard_map.91 = bf16[128,2048]{1,0:T(8,128)(2,1)S(1)} custom-call(s32[6]{0:T(128)S(1)} %copy-done.5, f32[4,6144]{1,0:T(4,128)S(1)} %copy-done.3, f32[1,2048]{1,0:T(1,128)S(1)} %bitcast.5, f32[16,16,128]{2,1,0:T(8,128)S(1)} %maximum_bitcast_fusion.scal_src, bf16[128,2048]{1,0:T(8,128)(2,1)S(1)} %copy-done, bf16[128,2048]{1,0:T(8,128)(2,1)S(1)} %copy-done.1, ...), custom_call_target="tpu_custom_call" | custom-call | tf_op jit(solution)/shard_map/pallas_call | solution.py:438
  58.6 0.8 %copy.12 = bf16[128,2048]{1,0:T(8,128)(2,1)} copy(bf16[128,2048]{1,0:T(8,128)(2,1)S(1)} %shard_map.91) | data formatting | bytes 1048576
  (1 shorter events, 0.0 us)
Async XLA Ops:
  0.1 0.9 %copy-start.6 = (f32[16,128]{1,0:T(8,128)S(1)}, f32[16,128]{1,0:T(8,128)}, u32[]{:S(2)}) copy-start(f32[16,128]{1,0:T(8,128)} %param.14) | copy-start | bytes 24580
  0.1 0.9 %copy-start.7 = (f32[16,128]{1,0:T(8,128)S(1)}, f32[16,128]{1,0:T(8,128)}, u32[]{:S(2)}) copy-start(f32[16,128]{1,0:T(8,128)} %param.13) | copy-start | bytes 24580
  1.0 0.9 %copy-start.3 = (f32[4,6144]{1,0:T(4,128)S(1)}, f32[4,6144]{1,0:T(4,128)}, u32[]{:S(2)}) copy-start(f32[4,6144]{1,0:T(4,128)} %cw_ref.1) | copy-start | bytes 294916
  1.0 0.9 %copy-start.4 = (f32[2048]{0:T(1024)S(1)}, f32[2048]{0:T(1024)}, u32[]{:S(2)}) copy-start(f32[2048]{0:T(1024)} %param.17) | copy-start | bytes 24580
  1.0 0.9 %copy-start.5 = (s32[6]{0:T(128)S(1)}, s32[6]{0:T(128)}, u32[]{:S(2)}) copy-start(s32[6]{0:T(128)} %doc_ref.1) | copy-start | bytes 76
  1.9 1.0 %copy-start = (bf16[128,2048]{1,0:T(8,128)(2,1)S(1)}, bf16[128,2048]{1,0:T(8,128)(2,1)}, u32[]{:S(2)}) copy-start(bf16[128,2048]{1,0:T(8,128)(2,1)} %q_src.1) | copy-start | bytes 1572868
  2.9 1.0 %copy-start.1 = (bf16[128,2048]{1,0:T(8,128)(2,1)S(1)}, bf16[128,2048]{1,0:T(8,128)(2,1)}, u32[]{:S(2)}) copy-start(bf16[128,2048]{1,0:T(8,128)(2,1)} %k_src.1) | copy-start | bytes 1572868
  4.0 1.0 %copy-start.2 = (bf16[128,2048]{1,0:T(8,128)(2,1)S(1)}, bf16[128,2048]{1,0:T(8,128)(2,1)}, u32[]{:S(2)}) copy-start(bf16[128,2048]{1,0:T(8,128)(2,1)} %v_src.1) | copy-start | bytes 1572868

commit v2 on v1

v2 whole, which is shorter than its diff:
```python
import functools
import jax
import jax.numpy as jnp
from jax import lax
from jax.experimental import pallas as pl
from jax.experimental.pallas import tpu as pltpu
from jax.sharding import PartitionSpec as P

F32 = jnp.float32
BF16 = jnp.bfloat16
C = 128
SEG = 16


def halves(x):
    high = x.astype(BF16)
    low = (x - high.astype(F32)).astype(BF16)
    return high, low


def left_form(x):
    return jnp.concatenate(halves(x), axis=1)


def twice(wide):
    return jnp.concatenate([wide, wide], axis=0)


def right_form(x):
    return twice(left_form(x))


def times(left, right):
    r = jnp.dot(left, right, preferred_element_type=F32)
    return r[:, :C] + r[:, C:]


def lanes_ds(i):
    return pl.ds(pl.multiple_of(i * C, C), C)


def fill_rows(first, doc_ref, msg_ref, rows_ref):
    bounds = []
    acc = jnp.int32(0)
    for i in range(doc_ref.shape[0]):
        bounds.append(acc)
        acc = acc + doc_ref[i]
    slab_pos = first + lax.broadcasted_iota(jnp.int32, (SEG, C), 0) * C
    pos = slab_pos + lax.broadcasted_iota(jnp.int32, (SEG, C), 1)

    def doc_of(p):
        total = jnp.zeros((SEG, C), F32)
        for b in bounds:
            total = total + jnp.where(p >= b, 1.0, 0.0)
        return total

    doc = doc_of(pos)
    upper = (lax.broadcasted_iota(jnp.int32, (C, C), 0) <= lax.broadcasted_iota(jnp.int32, (C, C), 1)).astype(F32)
    slabs = pl.ds(1, SEG)
    cum = jnp.dot(msg_ref[slabs, 0, :], upper, precision=lax.Precision.HIGHEST, preferred_element_type=F32)
    rows_ref[:, 0, :] = cum
    for r in range(1, 9):
        rows_ref[:, r, :] = msg_ref[slabs, r, :]
    rows_ref[:, 9, :] = doc
    rows_ref[:, 10, :] = jnp.where(doc == doc_of(slab_pos - 1), jnp.exp(cum), 0.0)
    for m in (1, 2, 3):
        rows_ref[:, 10 + m, :] = jnp.where(doc == doc_of(pos - m), 1.0, 0.0)
    rows_ref[:, 14, :] = jnp.zeros((SEG, C), F32)
    rows_ref[:, 15, :] = jnp.zeros((SEG, C), F32)


def conv(j, a, cols, taps_ref, x_ref, msg_ref):
    x = x_ref[j, a].astype(F32)
    before = msg_ref[j, 9 + 3 * a : 12 + 3 * a, :]
    total = taps_ref[a, 0:1, :] * x
    for m in (1, 2, 3):
        moved = jnp.concatenate([before[3 - m :], x[: C - m]], axis=0)
        total = total + taps_ref[a, m : m + 1, :] * moved * cols[:, 10 + m : 11 + m]
    return total / (1.0 + jnp.exp(-total))


def unit(x):
    return x * lax.rsqrt(jnp.sum(x * x, axis=1, keepdims=True) + 1e-06)


def slab_states(js, taps_ref, rows_ref, x_ref, msg_ref, kt_ref, inv_ref, v_ref, hk_ref, decay_ref, trans_ref, write_ref):
    above = lax.broadcasted_iota(jnp.int32, (C, C), 0)
    along = lax.broadcasted_iota(jnp.int32, (C, C), 1)
    lower = above >= along
    apart = jnp.where(above > along, above ^ along, 0)
    eye = jnp.where(above == along, 1.0, 0.0)
    n = len(js)
    k, cols, rows = [], [], []
    for j in js:
        r = rows_ref[j]
        c = r.T
        rows.append(r)
        cols.append(c)
        k.append(unit(conv(j, 1, c, taps_ref, x_ref, msg_ref)))
        v_ref[j] = left_form(conv(j, 2, c, taps_ref, x_ref, msg_ref))
    kt = [x.T for x in k]
    outer, system = [], []
    for i in range(n):
        wide = left_form(kt[i])
        kt_ref[js[i]] = wide
        r, c = rows[i], cols[i]
        gram = times(left_form(k[i]), twice(wide))
        hk_ref[js[i]] = left_form(k[i] * c[:, 10:11])
        keep = lower & (c[:, 9:10] == r[9:10])
        decay = jnp.exp(jnp.where(keep, c[:, 0:1] - r[0:1], -1e30)) * r[1:2]
        last = jnp.exp(jnp.where(keep[C - 1 : C], r[0:1, C - 1 : C] - r[0:1], -1e30)) * r[1:2]
        decay_ref[js[i]] = decay
        outer.append(kt[i] * last)
        system.append(decay * gram)
    inverse = [eye - jnp.where(apart == 1, system[i], 0.0) for i in range(n)]
    b = 2
    while b < C:
        pick = (apart >= b) & (apart < 2 * b)
        half = [times(left_form(inverse[i]), right_form(jnp.where(pick, system[i], 0.0))) for i in range(n)]
        inverse = [inverse[i] - times(left_form(half[i]), right_form(inverse[i])) for i in range(n)]
        b *= 2
    wide = [left_form(inverse[i]) for i in range(n)]
    for i in range(n):
        inv_ref[js[i]] = wide[i]
    mixed = [left_form(times(left_form(outer[i]), twice(wide[i]))) for i in range(n)]
    for i in range(n):
        write_ref[js[i]] = times(mixed[i], twice(v_ref[js[i]]))
        trans_ref[js[i]] = rows[i][10:11, C - 1 : C] * eye - times(mixed[i], twice(hk_ref[js[i]]))


def block_totals(trans_ref, write_ref, lev_ref, seg_ref):
    blocks = [(trans_ref[j], write_ref[j]) for j in range(SEG)]
    kept = 0
    while len(blocks) > 1:
        joined = []
        for a in range(0, len(blocks), 2):
            upper = left_form(blocks[a + 1][0])
            lower = [left_form(x) for x in blocks[a]]
            for part in (0, 1):
                lev_ref[kept, part] = lower[part]
            kept += 1
            joined.append((times(upper, twice(lower[0])), times(upper, twice(lower[1])) + blocks[a + 1][1]))
        blocks = joined
    seg_ref[0] = blocks[0][0]
    seg_ref[1] = blocks[0][1]


def level_reads(rows_ref, lev_ref, local_ref, reach_ref):
    kept = 0
    for level in range(1, 5):
        size = 1 << (level - 1)
        for first in range(size, SEG, 2 * size):
            at = pl.ds(first * C, size * C)
            reach = reach_ref[at, :]
            got = times(reach, twice(lev_ref[kept, 1]))
            for d in range(size):
                weight = rows_ref[first + d].T[:, 2 + level : 3 + level]
                local_ref[first + d] = local_ref[first + d] + got[d * C : (d + 1) * C] * weight
            reach_ref[at, :] = left_form(times(reach, twice(lev_ref[kept, 0])))
            kept += 1


def slab_reads(js, taps_ref, rows_ref, x_ref, msg_ref, kt_ref, inv_ref, v_ref, hk_ref, decay_ref, local_ref, reach_ref):
    n = len(js)
    q, cols = [], []
    for j in js:
        c = rows_ref[j].T
        cols.append(c)
        q.append(unit(conv(j, 0, c, taps_ref, x_ref, msg_ref)) * C ** (-0.5))
    attn = [left_form(times(left_form(q[i]), twice(kt_ref[js[i]])) * decay_ref[js[i]]) for i in range(n)]
    attn = [left_form(times(attn[i], twice(inv_ref[js[i]]))) for i in range(n)]
    for i in range(n):
        local_ref[js[i]] = times(attn[i], twice(v_ref[js[i]])) * cols[i][:, 2:3]
        qeff = q[i] * cols[i][:, 10:11] - times(attn[i], twice(hk_ref[js[i]]))
        reach_ref[pl.ds(pl.multiple_of(js[i] * C, C), C), :] = left_form(qeff)


def final(j, s5, s6, gain, rows_ref, local_ref, reach_ref):
    c = rows_ref[j].T
    reach = reach_ref[pl.ds(pl.multiple_of(j * C, C), C), :]
    o = local_ref[j] + times(reach, s5) * c[:, 7:8] + times(reach, s6) * c[:, 8:9]
    return (o * lax.rsqrt(jnp.mean(o * o, axis=1, keepdims=True) + 1e-06) * gain).astype(BF16)


def kernel(
    doc_src, cw_src, gain_src, gates_src, betas_src, weights_src, q_src, k_src, v_src, out_ref,
    doc_ref, taps_ref, gain_ref, raw_ref, tail_ref, pack_ref, msg_ref, x_ref, rows_ref,
    kt_ref, inv_ref, v_ref, hk_ref, decay_ref, trans_ref, write_ref, lev_ref, local_ref, reach_ref,
    seg_ref, far_ref, joint_ref, states_ref, stage_ref,
    load_sem, msg_send, msg_recv, edge_send, in_send, in_recv, far_send, far_recv, out_send, out_recv,
):
    me = lax.axis_index("ctx")
    segment = lax.div(me, SEG)
    mine = lax.rem(me, SEG)
    my_z, my_x, my_core = lax.div(mine, 8), lax.rem(lax.div(mine, 2), 4), lax.rem(mine, 2)
    sources = (q_src, k_src, v_src)

    loads = [
        pltpu.make_async_copy(gates_src, raw_ref.at[0], load_sem.at[0]),
        pltpu.make_async_copy(betas_src, raw_ref.at[1], load_sem.at[1]),
        pltpu.make_async_copy(weights_src, raw_ref.at[pl.ds(2, 7)], load_sem.at[2]),
    ]
    loads += [
        pltpu.make_async_copy(sources[a].at[pl.ds(C - 16, 16), :], tail_ref.at[a], load_sem.at[3 + a]) for a in range(3)
    ]
    small = [
        pltpu.make_async_copy(cw_src.at[:, lanes_ds(SEG * a + mine)], taps_ref.at[a], load_sem.at[6 + a]) for a in range(3)
    ]
    small += [
        pltpu.make_async_copy(gain_src.at[:, lanes_ds(mine)], gain_ref, load_sem.at[9]),
        pltpu.make_async_copy(doc_src, doc_ref, load_sem.at[10]),
    ]
    for copy in loads + small:
        copy.start()

    def place(dz, dx, dc):
        return lax.rem(my_z + dz, 2) * 8 + lax.rem(my_x + dx, 4) * 2 + lax.rem(my_core + dc, 2)

    def at(seg, head):
        return {"ctx": lax.rem(seg, 4) * SEG + head}

    barrier = pltpu.get_barrier_semaphore()

    def greet(target):
        pl.semaphore_signal(barrier, inc=1, device_id=target, device_id_type=pl.DeviceIdType.MESH)

    for n in range(1, 4):
        greet(at(segment + n, mine))
    greet(at(segment + 3, SEG - 1))
    for n in range(1, SEG):
        greet(at(segment, lax.rem(mine + n, SEG)))

    @pl.when(mine == SEG - 1)
    def _():
        for n in range(SEG):
            greet(at(segment + 1, n))

    def keeping(a):
        return pltpu.make_async_copy(sources[a].at[:, lanes_ds(mine)], x_ref.at[mine, a], in_recv.at[mine, a])

    for a in (1, 2, 0):
        keeping(a).start()
    for copy in loads:
        copy.wait()
    for r in range(9):
        pack_ref[:, r, :] = raw_ref[r]
    for h in range(SEG):
        for a in range(3):
            pack_ref[h, 9 + 3 * a : 12 + 3 * a, :] = tail_ref[a, 8:16, h * C : (h + 1) * C].astype(F32)[5:8]
    for r in range(18, 24):
        pack_ref[:, r, :] = jnp.zeros((SEG, C), F32)

    @pl.when(mine == SEG - 1)
    def _():
        pl.semaphore_wait(barrier, 19 + SEG)

    @pl.when(mine != SEG - 1)
    def _():
        pl.semaphore_wait(barrier, 19)

    order = [(dz, dx, dc) for dx in (0, 1, 3, 2) for dz in (0, 1) for dc in (0, 1)][1:]

    def message(head):
        return pltpu.make_async_remote_copy(
            src_ref=pack_ref.at[head], dst_ref=msg_ref.at[mine + 1],
            send_sem=msg_send.at[head], recv_sem=msg_recv.at[mine + 1],
            device_id=at(segment, head), device_id_type=pl.DeviceIdType.MESH,
        )

    def message_from(slab):
        return pltpu.make_async_remote_copy(
            src_ref=pack_ref.at[slab], dst_ref=msg_ref.at[slab + 1],
            send_sem=msg_send.at[slab], recv_sem=msg_recv.at[slab + 1],
            device_id=at(segment, slab), device_id_type=pl.DeviceIdType.MESH,
        )

    own_message = pltpu.make_async_copy(pack_ref.at[mine], msg_ref.at[mine + 1], msg_recv.at[mine + 1])

    def edge(head):
        return pltpu.make_async_remote_copy(
            src_ref=pack_ref.at[head], dst_ref=msg_ref.at[0],
            send_sem=edge_send.at[head], recv_sem=msg_recv.at[0],
            device_id=at(segment + 1, head), device_id_type=pl.DeviceIdType.MESH,
        )

    def sending(a, head):
        return pltpu.make_async_remote_copy(
            src_ref=sources[a].at[:, lanes_ds(head)], dst_ref=x_ref.at[mine, a],
            send_sem=in_send.at[head, a], recv_sem=in_recv.at[mine, a],
            device_id=at(segment, head), device_id_type=pl.DeviceIdType.MESH,
        )

    def arriving(a, slab):
        return pltpu.make_async_remote_copy(
            src_ref=sources[a].at[:, lanes_ds(slab)], dst_ref=x_ref.at[slab, a],
            send_sem=in_send.at[slab, a], recv_sem=in_recv.at[slab, a],
            device_id=at(segment, slab), device_id_type=pl.DeviceIdType.MESH,
        )

    own_message.start()
    for step in order:
        message(place(*step)).start()

    @pl.when(mine == SEG - 1)
    def _():
        for n in range(SEG):
            edge(jnp.int32(n)).start()

    for step in order:
        for a in (1, 2):
            sending(a, place(*step)).start()
    for step in order:
        sending(0, place(*step)).start()

    for copy in small:
        copy.wait()
    own_message.wait()
    for step in order:
        message_from(place(*step)).wait_recv()
    edge(mine).wait_recv()
    fill_rows(segment * (SEG * C), doc_ref, msg_ref, rows_ref)

    def members(m):
        dx = m + lax.div(m, 2) - 2 * lax.div(m, 3)
        x = lax.rem(my_x + 4 - dx, 4)
        return [z * 8 + x * 2 + core for z in (0, 1) for core in (0, 1)]

    def await_inputs(js, arrays):
        for j in js:
            @pl.when(j == mine)
            def _():
                for a in arrays:
                    keeping(a).wait()

            @pl.when(j != mine)
            def _():
                for a in arrays:
                    arriving(a, j).wait_recv()

    def state_group(m, _):
        js = members(m)
        await_inputs(js, (1, 2))
        slab_states(
            js, taps_ref, rows_ref, x_ref, msg_ref, kt_ref, inv_ref, v_ref, hk_ref, decay_ref, trans_ref, write_ref
        )
        return 0

    lax.fori_loop(0, 4, state_group, 0)

    def across(n, src, to, slot):
        return pltpu.make_async_remote_copy(
            src_ref=src, dst_ref=far_ref.at[slot], send_sem=far_send.at[n], recv_sem=far_recv.at[slot],
            device_id=at(jnp.int32(to), mine), device_id_type=pl.DeviceIdType.MESH,
        )

    block_totals(trans_ref, write_ref, lev_ref, seg_ref)
    first_write = across(0, seg_ref.at[1], 1, 0)
    third_trans = across(1, seg_ref.at[0], 3, 1)
    third_write = across(2, seg_ref.at[1], 3, 2)
    to_third = across(3, joint_ref, 2, 3)
    to_fourth = across(4, joint_ref, 3, 3)

    @pl.when(segment == 0)
    def _():
        first_write.start()

    @pl.when(segment == 2)
    def _():
        third_trans.start()
        third_write.start()

    states_ref[...] = jnp.zeros_like(states_ref)

    def read_group(m, _):
        @pl.when((segment == 1) & (m == 3))
        def _():
            first_write.wait_recv()
            states_ref[0] = far_ref[0]
            joint_ref[...] = times(left_form(seg_ref[0]), right_form(far_ref[0])) + seg_ref[1]
            to_fourth.start()
            to_third.start()

        js = members(m)
        await_inputs(js, (0,))
        slab_reads(
            js, taps_ref, rows_ref, x_ref, msg_ref,
            kt_ref, inv_ref, v_ref, hk_ref, decay_ref, local_ref, reach_ref,
        )
        return 0

    lax.fori_loop(0, 4, read_group, 0)
    level_reads(rows_ref, lev_ref, local_ref, reach_ref)

    @pl.when(segment == 2)
    def _():
        to_third.wait_recv()
        states_ref[1] = far_ref[3]

    @pl.when(segment == 3)
    def _():
        third_trans.wait_recv()
        third_write.wait_recv()
        states_ref[0] = far_ref[2]
        to_fourth.wait_recv()
        states_ref[1] = times(left_form(far_ref[1]), right_form(far_ref[3]))

    gain = gain_ref[...]
    s5 = right_form(states_ref[0])
    s6 = right_form(states_ref[1])

    def leaving(slab):
        return pltpu.make_async_remote_copy(
            src_ref=stage_ref.at[slab], dst_ref=out_ref.at[:, lanes_ds(mine)],
            send_sem=out_send.at[slab], recv_sem=out_recv.at[mine],
            device_id=at(segment, slab), device_id_type=pl.DeviceIdType.MESH,
        )

    def returning(head):
        return pltpu.make_async_remote_copy(
            src_ref=stage_ref.at[head], dst_ref=out_ref.at[:, lanes_ds(head)],
            send_sem=out_send.at[head], recv_sem=out_recv.at[head],
            device_id=at(segment, head), device_id_type=pl.DeviceIdType.MESH,
        )

    for dx in (2, 1, 3, 0):
        js = [place(dz, dx, dc) for dz in (1, 0) for dc in (1, 0)]
        for j in js:
            stage_ref[j] = final(j, s5, s6, gain, rows_ref, local_ref, reach_ref)
        for j in js[: 4 if dx else 3]:
            leaving(j).start()
    home = pltpu.make_async_copy(stage_ref.at[mine], out_ref.at[:, lanes_ds(mine)], out_recv.at[mine])
    home.start()
    home.wait()
    for step in order:
        returning(place(*step)).wait_recv()

    for step in order:
        head = place(*step)
        message(head).wait_send()
        for a in range(3):
            sending(a, head).wait_send()
        leaving(head).wait_send()

    @pl.when(mine == SEG - 1)
    def _():
        for n in range(SEG):
            edge(jnp.int32(n)).wait_send()

    @pl.when(segment == 0)
    def _():
        first_write.wait_send()

    @pl.when(segment == 1)
    def _():
        to_third.wait_send()
        to_fourth.wait_send()

    @pl.when(segment == 2)
    def _():
        third_trans.wait_send()
        third_write.wait_send()


def body(queries, keys, values_in, conv_weights, log_gates, betas, level_weights, doc_lengths, out_gain):
    square = pltpu.VMEM((SEG, C, C), F32)
    wide = pltpu.VMEM((SEG, C, 2 * C), BF16)
    hbm = pl.BlockSpec(memory_space=pl.ANY)
    dma = pltpu.SemaphoreType.DMA
    return pl.pallas_call(
        kernel,
        out_shape=jax.ShapeDtypeStruct(queries.shape, BF16),
        in_specs=[hbm] * 9,
        out_specs=hbm,
        scratch_shapes=[
            pltpu.SMEM(doc_lengths.shape, jnp.int32),
            pltpu.VMEM((3, 4, C), F32),
            pltpu.VMEM((1, C), F32),
            pltpu.VMEM((9, SEG, C), F32),
            pltpu.VMEM((3, 16, queries.shape[1]), BF16),
            pltpu.VMEM((SEG, 24, C), F32),
            pltpu.VMEM((SEG + 1, 24, C), F32),
            pltpu.VMEM((SEG, 3, C, C), BF16),
            pltpu.VMEM((SEG, 16, C), F32),
            wide, wide, wide, wide, square, square, square,
            pltpu.VMEM((SEG - 1, 2, C, 2 * C), BF16),
            square,
            pltpu.VMEM((SEG * C, 2 * C), BF16),
            pltpu.VMEM((2, C, C), F32),
            pltpu.VMEM((4, C, C), F32),
            pltpu.VMEM((C, C), F32),
            pltpu.VMEM((2, C, C), F32),
            pltpu.VMEM((SEG, C, C), BF16),
            dma((11,)), dma((SEG,)), dma((SEG + 1,)), dma((SEG,)), dma((SEG, 3)), dma((SEG, 3)),
            dma((5,)), dma((4,)), dma((SEG,)), dma((SEG,)),
        ],
        compiler_params=pltpu.CompilerParams(
            collective_id=0, has_side_effects=True, vmem_limit_bytes=60 << 20
        ),
    )(
        doc_lengths, conv_weights, out_gain[None, :], log_gates, betas, level_weights, queries, keys, values_in
    )


def solution(mesh):
    in_specs = (
        P(("dp", "ctx"), None),
        P(("dp", "ctx"), None),
        P(("dp", "ctx"), None),
        P(),
        P(None, ("dp", "ctx")),
        P(None, ("dp", "ctx")),
        P(None, None, ("dp", "ctx")),
        P("dp"),
        P(),
    )
    out_specs = P(("dp", "ctx"), None)
    return jax.shard_map(body, mesh=mesh, in_specs=in_specs, out_specs=out_specs, check_vma=False)
```

time: 60.6 us -> 51.7 us (0.85); the launches traced: 59.4 us -> 51.6 us
  Pallas kernels: 53.6 us -> 49.7 us
  local copies, waits for them, and re-layouts: 5.67 us -> 1.88 us
    pallas_call x1, Pallas kernels: 53.6 us -> 49.7 us  [body(): pl.pallas_call(kernel, out_shape=jax.ShapeDtypeStruct(queries.shape, BF16...]
    unnamed x18 -> x1, local copies, waits for them, and re-layouts: 5.59 us -> 1.88 us
where the time goes in v2:
time: 51.7 us; the launch traced here: 51.6 us
  Pallas kernels  49.7 us (96%)
  local copies, waits for them, and re-layouts  1.88 us (4%)
    pallas_call x1, Pallas kernels, body(): pl.pallas_call(kernel, out_shape=jax.ShapeDtypeStruct(queries.shape, BF16...  49.7 us
    unnamed x1, local copies, waits for them, and re-layouts  1.88 us

profile of v2, /device:TPU:1, one launch (start us, length us, event | category | flops | bytes accessed | tf_op | source)
XLA Modules:
  0.0 51.6 jit_solution(11829674360131714509)
XLA Ops:
  0.0 49.7 %shard_map.91 = bf16[128,2048]{1,0:T(8,128)(2,1)} custom-call(s32[6]{0:T(128)} %doc_src.1, f32[4,6144]{1,0:T(4,128)} %cw_src.1, f32[1,2048]{1,0:T(1,128)} %bitcast.1, f32[16,128]{1,0:T(8,128)} %gates_src.1, f32[16,128]{1,0:T(8,128)} %betas_src.1, f32[7,16,128]{2,1,0:T(8,128)} %weights_src.1, bf16[128,2048]{1,0:T(8,128)(2,1)} %q_src.1, ...), custom_call_target="tpu_custom_call" | custom-call | tf_op jit(solution)/shard_map/pallas_call | solution.py:469
  49.7 1.9 %copy.11 = bf16[128,2048]{1,0:T(8,128)(2,1)} copy(bf16[128,2048]{1,0:T(8,128)(2,1)} %shard_map.91) | data formatting | bytes 1048576

commit v3 on v2

--- a/solution.py
+++ b/solution.py
@@ -338,14 +338,14 @@
                     arriving(a, j).wait_recv()
 
     def state_group(m, _):
-        js = members(m)
+        js = members(2 * m) + members(2 * m + 1)
         await_inputs(js, (1, 2))
         slab_states(
             js, taps_ref, rows_ref, x_ref, msg_ref, kt_ref, inv_ref, v_ref, hk_ref, decay_ref, trans_ref, write_ref
         )
         return 0
 
-    lax.fori_loop(0, 4, state_group, 0)
+    lax.fori_loop(0, 2, state_group, 0)
 
     def across(n, src, to, slot):
         return pltpu.make_async_remote_copy(
@@ -372,7 +372,7 @@
     states_ref[...] = jnp.zeros_like(states_ref)
 
     def read_group(m, _):
-        @pl.when((segment == 1) & (m == 3))
+        @pl.when((segment == 1) & (m == 1))
         def _():
             first_write.wait_recv()
             states_ref[0] = far_ref[0]
@@ -380,7 +380,7 @@
             to_fourth.start()
             to_third.start()
 
-        js = members(m)
+        js = members(2 * m) + members(2 * m + 1)
         await_inputs(js, (0,))
         slab_reads(
             js, taps_ref, rows_ref, x_ref, msg_ref,
@@ -388,7 +388,7 @@
         )
         return 0
 
-    lax.fori_loop(0, 4, read_group, 0)
+    lax.fori_loop(0, 2, read_group, 0)
     level_reads(rows_ref, lev_ref, local_ref, reach_ref)
 
     @pl.when(segment == 2)

time: 51.7 us -> 51.7 us (level)
  no operation moved by 1% of the time
where the time goes in v3:
time: 51.7 us; the launch traced here: 51.5 us
  Pallas kernels  49.6 us (96%)
  local copies, waits for them, and re-layouts  1.88 us (4%)
    pallas_call x1, Pallas kernels, body(): pl.pallas_call(kernel, out_shape=jax.ShapeDtypeStruct(queries.shape, BF16...  49.6 us
    unnamed x1, local copies, waits for them, and re-layouts  1.88 us

profile of v3, /device:TPU:1, one launch (start us, length us, event | category | flops | bytes accessed | tf_op | source)
XLA Modules:
  0.0 51.5 jit_solution(7384634112566074396)
XLA Ops:
  0.0 49.6 %shard_map.91 = bf16[128,2048]{1,0:T(8,128)(2,1)} custom-call(s32[6]{0:T(128)} %doc_src.1, f32[4,6144]{1,0:T(4,128)} %cw_src.1, f32[1,2048]{1,0:T(1,128)} %bitcast.1, f32[16,128]{1,0:T(8,128)} %gates_src.1, f32[16,128]{1,0:T(8,128)} %betas_src.1, f32[7,16,128]{2,1,0:T(8,128)} %weights_src.1, bf16[128,2048]{1,0:T(8,128)(2,1)} %q_src.1, ...), custom_call_target="tpu_custom_call" | custom-call | tf_op jit(solution)/shard_map/pallas_call | solution.py:469
  49.6 1.9 %copy.11 = bf16[128,2048]{1,0:T(8,128)(2,1)} copy(bf16[128,2048]{1,0:T(8,128)(2,1)} %shard_map.91) | data formatting | bytes 1048576

commit v4 on v3

--- a/solution.py
+++ b/solution.py
@@ -337,15 +337,18 @@
                 for a in arrays:
                     arriving(a, j).wait_recv()
 
-    def state_group(m, _):
-        js = members(2 * m) + members(2 * m + 1)
+    def state_group(js):
         await_inputs(js, (1, 2))
         slab_states(
             js, taps_ref, rows_ref, x_ref, msg_ref, kt_ref, inv_ref, v_ref, hk_ref, decay_ref, trans_ref, write_ref
         )
+
+    def early(m, _):
+        state_group(members(m))
         return 0
 
-    lax.fori_loop(0, 2, state_group, 0)
+    lax.fori_loop(0, 2, early, 0)
+    state_group(members(jnp.int32(2)) + members(jnp.int32(3)))
 
     def across(n, src, to, slot):
         return pltpu.make_async_remote_copy(

time: 51.7 us -> 51.6 us (level)
  no operation moved by 1% of the time
where the time goes in v4:
time: 51.6 us; the launch traced here: 51.4 us
  Pallas kernels  49.5 us (96%)
  local copies, waits for them, and re-layouts  1.88 us (4%)
    pallas_call x1, Pallas kernels, body(): pl.pallas_call(kernel, out_shape=jax.ShapeDtypeStruct(queries.shape, BF16...  49.5 us
    unnamed x1, local copies, waits for them, and re-layouts  1.88 us

profile of v4, /device:TPU:1, one launch (start us, length us, event | category | flops | bytes accessed | tf_op | source)
XLA Modules:
  0.0 51.4 jit_solution(5721078147434796966)
XLA Ops:
  0.0 49.5 %shard_map.91 = bf16[128,2048]{1,0:T(8,128)(2,1)} custom-call(s32[6]{0:T(128)} %doc_src.1, f32[4,6144]{1,0:T(4,128)} %cw_src.1, f32[1,2048]{1,0:T(1,128)} %bitcast.1, f32[16,128]{1,0:T(8,128)} %gates_src.1, f32[16,128]{1,0:T(8,128)} %betas_src.1, f32[7,16,128]{2,1,0:T(8,128)} %weights_src.1, bf16[128,2048]{1,0:T(8,128)(2,1)} %q_src.1, ...), custom_call_target="tpu_custom_call" | custom-call | tf_op jit(solution)/shard_map/pallas_call | solution.py:472
  49.5 1.9 %copy.11 = bf16[128,2048]{1,0:T(8,128)(2,1)} copy(bf16[128,2048]{1,0:T(8,128)(2,1)} %shard_map.91) | data formatting | bytes 1048576
